TPU v7x, 256 devices: a whole 4x4x8 slice. The times are simulated.
256 devices in a mesh: row: 32 (over y, x, core), col: 8 (over z).
Axes of the slice: x: 4, y: 4, z: 8, core: 2. Of those that a mesh axis runs over, the one named last changes fastest.
Arguments:
- hidden: bfloat16 [2048, 2560], P(None, 'row'), may hold values from -6 to 6
- w_qkv: bfloat16 [2560, 3584], P('row', 'col'), may hold values from -8 to 8
- page_table: int32 [64, 64], P('row'), may hold values from -1 to 127, as said below
- prompt_lengths: int32 [64], P('row'), may hold values from 1 to 8192, as said below
- page_keys: bfloat16 [32, 128, 128, 512], P('row', 'col'), may hold values from -4 to 4
- page_values: bfloat16 [32, 128, 128, 512], P('row', 'col'), may hold values from -6 to 6
- tail_lengths: int32 [64, 16], P('row'), may hold values from 0 to 512
- tail_keys: bfloat16 [64, 16, 512, 512], P('row', 'col'), may hold values from -6 to 6
- tail_values: bfloat16 [64, 16, 512, 512], P('row', 'col'), may hold values from -6 to 6
Outputs:
- attended: bfloat16 [64, 16, 2, 2560], P('row', 'col')
Inputs may be any that keep to these rules, and one draw needn't show every extreme that they name: `page_table`: entry j of prompt p is the slot of block p // 2 that holds its tokens j * 128 to (j + 1) * 128 - 1 where j * 128 < prompt_lengths[p], else -1; the live slots of a block are distinct. Slot k of a block lies on the device of col index k // 16. The live pages of a block fill the devices' slots one device after another, in an order drawn from the seed, so that at least one device holds 16 live pages. `prompt_lengths`: every block of 2 prompts holds a prompt of 8192 tokens.
All inputs are finite; a program needn't handle non-finite values.
Results may differ from a plain program's by a relative error of at most 0.015.
The roundings to bfloat16 on the way count: a program that leaves them out, or rounds other values in their place, can miss the bound.
Values may be sent and summed in bfloat16 or wider, within the bound.
A program may use at most 64 MiB of HBM per device.

v0:
```python
import math

import jax
import jax.numpy as jnp
from jax import lax
from jax.sharding import PartitionSpec as P

HEADS = 20
KVH = 4
HD = 128
SAMPLES = 16


rope_base = 500000.0
masked_score = -1e30


def merged(value, axis, join):
    pieces = jax.tree.map(lambda part: lax.all_gather(part, axis), value)
    head = jax.tree.map(lambda part: part[0], pieces)
    tail = jax.tree.map(lambda part: part[1:], pieces)
    total, _ = lax.scan(lambda total, section: (join(total, section), None), head, tail)
    return total


def rotate(vectors, positions):
    half_size = vectors.shape[-1] // 2
    frequency = jnp.exp(
        jnp.arange(half_size, dtype=jnp.float32) * (-2.0 * math.log(rope_base) / vectors.shape[-1])
    )
    angles = positions.astype(jnp.float32)[..., None, None] * frequency
    cosine = jnp.cos(angles)
    sines = jnp.sin(angles)
    leading = vectors[..., :half_size].astype(jnp.float32)
    trailing = vectors[..., half_size:].astype(jnp.float32)
    return jnp.concatenate(
        [leading * cosine - trailing * sines, trailing * cosine + leading * sines], axis=-1
    )


def combine_states(earlier, later):
    top_early, sums_early, acc_early = earlier
    top_late, sums_late, acc_late = later
    highest = jnp.maximum(top_early, top_late)
    scale_early = jnp.exp(top_early - highest)
    scale_late = jnp.exp(top_late - highest)
    return (
        highest,
        sums_early * scale_early + sums_late * scale_late,
        acc_early * scale_early[..., None] + acc_late * scale_late[..., None],
    )


def project_rows(hidden, weights):
    return jnp.dot(hidden, weights, preferred_element_type=jnp.float32)


def local(
    hidden,
    w_qkv,
    page_table,
    prompt_lengths,
    page_keys,
    page_values,
    tail_lengths,
    tail_keys,
    tail_values,
):
    group_size = HEADS // KVH
    q_width = HEADS * HD
    kv_width = KVH * HD
    score_scale = 1.0 / math.sqrt(HD)
    column_sums = lax.psum_scatter(
        project_rows(hidden, w_qkv), "row", scatter_dimension=0, tiled=True
    ).astype(jnp.bfloat16)
    projected = lax.all_gather(column_sums, "col", axis=1, tiled=True)
    prompts_here = prompt_lengths.shape[0]
    projected = projected.reshape(prompts_here, SAMPLES, 2, projected.shape[-1])
    steps_ahead = jnp.arange(2, dtype=jnp.int32)
    positions = (
        prompt_lengths[:, None, None] + tail_lengths[:, :, None] + steps_ahead[None, None, :]
    )
    queries = rotate(
        projected[..., :q_width].reshape(prompts_here, SAMPLES, 2, HEADS, HD), positions
    ).astype(jnp.bfloat16)
    new_keys = rotate(
        projected[..., q_width : q_width + kv_width].reshape(prompts_here, SAMPLES, 2, KVH, HD),
        positions,
    ).astype(jnp.bfloat16)
    new_values = projected[..., q_width + kv_width :].reshape(prompts_here, SAMPLES, 2, KVH, HD)
    pool_keys = page_keys[0]
    pool_values = page_values[0]
    pool_slots = pool_keys.shape[0]
    page_size = pool_keys.shape[1]
    slot_ids = lax.axis_index("col") * pool_slots + jnp.arange(pool_slots, dtype=jnp.int32)
    matches = (page_table[None, :, :] == slot_ids[:, None, None]).astype(jnp.int32)
    owners = jnp.sum(matches, axis=2)
    page_index = jnp.sum(
        matches * jnp.arange(page_table.shape[1], dtype=jnp.int32)[None, None, :], axis=(1, 2)
    )
    slot_prompt = jnp.sum(owners * jnp.arange(prompts_here, dtype=jnp.int32)[None, :], axis=1)
    slot_length = jnp.sum(owners * prompt_lengths[None, :], axis=1)
    key_positions = (
        page_index[:, None] * page_size + jnp.arange(page_size, dtype=jnp.int32)[None, :]
    )
    visible = (key_positions < slot_length[:, None])[:, None, None, None, :]
    query_grid = queries.reshape(prompts_here, SAMPLES * 2, KVH, group_size, HD)
    slot_queries = jnp.take(query_grid, slot_prompt, axis=0)
    page_scores = (
        jnp.einsum(
            "sqkgd,spkd->sqkgp",
            slot_queries,
            pool_keys.reshape(pool_slots, page_size, KVH, HD),
            preferred_element_type=jnp.float32,
        )
        * score_scale
    )
    page_scores = jnp.where(visible, page_scores, masked_score)
    slot_top = jnp.max(page_scores, axis=-1)
    prompt_top = jnp.max(
        jnp.where(owners[:, :, None, None, None] > 0, slot_top[:, None], masked_score), axis=0
    )
    slot_shift = jnp.take(prompt_top, slot_prompt, axis=0)
    page_weights = jnp.where(visible, jnp.exp(page_scores - slot_shift[..., None]), 0.0)
    slot_sums = jnp.sum(page_weights, axis=-1)
    slot_acc = jnp.einsum(
        "sqkgp,spkd->sqkgd",
        page_weights.astype(jnp.bfloat16),
        pool_values.reshape(pool_slots, page_size, KVH, HD),
        preferred_element_type=jnp.float32,
    )
    owner_float = owners.astype(jnp.float32)
    prefix_sums = jnp.einsum(
        "sr,sqkg->rqkg", owner_float, slot_sums, precision=lax.Precision.HIGHEST
    )
    prefix_acc = jnp.einsum(
        "sr,sqkgd->rqkgd", owner_float, slot_acc, precision=lax.Precision.HIGHEST
    )
    state_shape = (prompts_here, SAMPLES, 2, KVH, group_size)
    prefix_top = prompt_top.reshape(state_shape)
    prefix_sums = prefix_sums.reshape(state_shape)
    prefix_acc = prefix_acc.reshape(state_shape + (HD,))
    own_count = tail_keys.shape[1]
    own_start = lax.axis_index("col") * own_count
    whole_top, whole_sums, whole_acc = merged(
        (prefix_top, prefix_sums, prefix_acc), "col", combine_states
    )
    merged_top = lax.dynamic_slice_in_dim(whole_top, own_start, own_count, 1)
    merged_sums = lax.dynamic_slice_in_dim(whole_sums, own_start, own_count, 1)
    merged_acc = lax.dynamic_slice_in_dim(whole_acc, own_start, own_count, 1)
    own_queries = lax.dynamic_slice_in_dim(queries, own_start, own_count, 1).reshape(
        prompts_here, own_count, 2, KVH, group_size, HD
    )
    own_keys = lax.dynamic_slice_in_dim(new_keys, own_start, own_count, 1)
    own_values = lax.dynamic_slice_in_dim(new_values, own_start, own_count, 1)
    own_tails = lax.dynamic_slice_in_dim(tail_lengths, own_start, own_count, 1)
    tail_room = tail_keys.shape[2]
    tail_grid = tail_keys.reshape(prompts_here, own_count, tail_room, KVH, HD)
    tail_scores = (
        jnp.einsum(
            "rstkgd,rsjkd->rstkgj", own_queries, tail_grid, preferred_element_type=jnp.float32
        )
        * score_scale
    )
    tail_seen = (jnp.arange(tail_room, dtype=jnp.int32)[None, None, :] < own_tails[:, :, None])[
        :, :, None, None, None, :
    ]
    tail_scores = jnp.where(tail_seen, tail_scores, masked_score)
    fresh_scores = (
        jnp.einsum(
            "rstkgd,rsukd->rstkgu", own_queries, own_keys, preferred_element_type=jnp.float32
        )
        * score_scale
    )
    causal = (steps_ahead[None, :] <= steps_ahead[:, None])[None, None, :, None, None, :]
    fresh_scores = jnp.where(causal, fresh_scores, masked_score)
    local_top = jnp.maximum(jnp.max(tail_scores, axis=-1), jnp.max(fresh_scores, axis=-1))
    tail_weights = jnp.where(tail_seen, jnp.exp(tail_scores - local_top[..., None]), 0.0)
    fresh_weights = jnp.where(causal, jnp.exp(fresh_scores - local_top[..., None]), 0.0)
    local_sums = jnp.sum(tail_weights, axis=-1) + jnp.sum(fresh_weights, axis=-1)
    local_acc = jnp.einsum(
        "rstkgj,rsjkd->rstkgd",
        tail_weights.astype(jnp.bfloat16),
        tail_values.reshape(prompts_here, own_count, tail_room, KVH, HD),
        preferred_element_type=jnp.float32,
    )
    local_acc = local_acc + jnp.einsum(
        "rstkgu,rsukd->rstkgd",
        fresh_weights.astype(jnp.bfloat16),
        own_values,
        preferred_element_type=jnp.float32,
    )
    final_top, final_sums, final_acc = combine_states(
        (merged_top, merged_sums, merged_acc), (local_top, local_sums, local_acc)
    )
    attended = final_acc / final_sums[..., None]
    return attended.reshape(prompts_here, own_count, 2, HEADS * HD).astype(jnp.bfloat16)


def solution(mesh):
    in_specs = (
        P(None, "row"),
        P("row", "col"),
        P("row", None),
        P("row"),
        P("row", "col", None, None),
        P("row", "col", None, None),
        P("row", None),
        P("row", "col", None, None),
        P("row", "col", None, None),
    )
    out_specs = P("row", "col", None, None)
    return jax.shard_map(local, mesh=mesh, in_specs=in_specs, out_specs=out_specs, check_vma=False)
```

profile of v0, /device:TPU:6, one launch (start us, length us, event | category | flops | bytes accessed | tf_op | source)
XLA Modules:
  0.0 266.6 jit_solution(7269477015864981519)
XLA Ops:
  7.5 3.6 %fusion.110 = f32[2048,448]{1,0:T(8,128)} fusion(bf16[2048,80]{0,1:T(8,128)(2,1)S(1)} %copy-done, bf16[80,448]{1,0:T(8,128)(2,1)} %param.12), kind=kOutput, calls=%fused_computation.142 | convolution fusion | flops 146800640 | bytes 4069376 | tf_op jit(solution)/shard_map/dot_general | solution.py:55
  11.2 2.1 reshape_squeeze.6
  13.3 4.0 %reshape_squeeze.7 = bf16[16,128,4,128]{3,2,1,0:T(4,128)(2,1)} reshape(bf16[1,16,128,512]{3,2,1,0:T(8,128)(2,1)} %param.16) | data formatting | bytes 4194304 | tf_op jit(solution)/shard_map/reshape;squeeze | solution.py:129
  18.0 85.4 %reduce-scatter.2.cloned.1.call-done = f32[64,448]{1,0:T(8,128)} async-done(((f32[2048,448]{1,0:T(8,128)}), f32[64,448]{1,0:T(8,128)}) %reduce-scatter.2.cloned.1.call-update) | async-done | bytes 114704 | tf_op jit(solution)/shard_map/reduce_scatter | solution.py:73
  104.4 26.7 %all-gather.1 = bf16[8,448,64]{1,2,0:T(8,128)(2,1)S(1)} all-gather(bf16[1,448,64]{1,2,0:T(8,128)(2,1)S(1)} %convert_bitcast_fusion), channel_id=1, replica_groups=mesh['row'=32,'col'=8] {'col'}, dimensions={0}, use_global_device_ids=true | all-gather | bytes 516096 | tf_op jit(solution)/shard_map/all_gather | solution.py:76
  135.0 1.1 gather_fusion
  136.1 5.7 %bitcast_reduce_fusion = (f32[16,32,4,5]{1,3,2,0:T(8,128)S(1)}, f32[16,4,32,5,128]{4,2,3,1,0:T(8,128)}) fusion(pred[16,128]{1,0:T(8,128)(4,1)S(1)} %add_compare_fusion, bf16[16,128,4,128,1]{3,2,1,0,4:T(4,128)(2,1)} %bitcast.114, bf16[16,32,4,5,128]{4,1,3,2,0:T(8,128)(2,1)S(1)} %gather_fusion, pred[16]{0:T(512)(128)(4,1)S(1)} %compare_and_fusion), kind=kOutput, calls=%fused_computation.13 | convolution fusion | flops 340776960 | bytes 10004496 | tf_op jit(solution)/shard_map/sqkgd,spkd->sqkgp/dot_general | solution.py:110
  142.8 4.2 %fusion.21 = f32[16,32,4,5,128]{4,1,3,2,0:T(8,128)S(1)} fusion(f32[16,4,32,5,128]{4,2,3,1,0:T(8,128)} %get-tuple-element.131, f32[16,32,4,5]{1,3,2,0:T(8,128)S(1)} %copy.180, pred[16,128]{1,0:T(8,128)(4,1)S(1)} %add_compare_fusion, bf16[16,128,4,128,1]{3,2,1,0,4:T(4,128)(2,1)} %bitcast.113), kind=kOutput, calls=%fused_computation.31 | convolution fusion | flops 342097920 | bytes 12625920 | tf_op jit(solution)/shard_map/sqkgp,spkd->sqkgd/dot_general | solution.py:126
  147.0 7.4 %fusion.6 = f32[2,32,4,5,128]{4,0,3,2,1:T(2,128)S(1)} fusion(f32[16,32,4,5,128]{4,1,3,2,0:T(8,128)S(1)} %fusion.21, s32[16,2]{0,1:T(2,128)S(1)} %get-tuple-element.90), kind=kOutput, calls=%fused_computation.16 | convolution fusion | flops 31457312 | bytes 5898368 | tf_op jit(solution)/shard_map/sr,sqkgd->rqkgd/dot_general | solution.py:136
  154.4 1.0 copy.186
  155.5 2.6 reshape.151
  158.0 4.0 %reshape.153 = bf16[2,2,512,4,128]{4,3,2,1,0:T(4,128)(2,1)} reshape(bf16[2,2,512,512]{3,2,1,0:T(8,128)(2,1)} %param.19) | data formatting | bytes 4194304 | tf_op jit(solution)/shard_map/reshape | solution.py:184
  163.0 5.9 %fusion.9 = f32[16,32,4,5]{1,3,2,0:T(8,128)} fusion(f32[16,4,32,5,128]{4,2,3,1,0:T(8,128)} %get-tuple-element.131, f32[16,32,4,5]{1,3,2,0:T(8,128)S(1)} %copy.180, pred[16,128]{1,0:T(8,128)(4,1)S(1)} %add_compare_fusion), kind=kLoop, calls=%fused_computation.20 | loop fusion | flops 6543360 | bytes 5326848 | tf_op jit(solution)/shard_map/reduce_sum | solution.py:125
  168.8 1.1 copy.181
  170.0 2.4 fusion.66
  172.4 26.0 %all-gather = f32[16,16,2,4,5]{1,3,4,2,0:T(4,128)S(1)} all-gather(f32[2,16,2,4,5]{1,3,4,2,0:T(4,128)S(1)} %copy.183), channel_id=2, replica_groups=mesh['row'=32,'col'=8] {'col'}, dimensions={0}, use_global_device_ids=true | all-gather | bytes 46080 | tf_op jit(solution)/shard_map/all_gather | solution.py:19
  198.4 1.6 fusion.105
  200.0 1.5 reshape.185
  201.6 1.1 copy.178
  202.7 26.0 %all_gather.13 = f32[8,2,16,2,4,5]{2,4,5,3,1,0:T(4,128)S(1)} all-gather(f32[1,2,16,2,4,5]{2,4,5,3,1,0:T(4,128)S(1)} %copy.178), channel_id=1, replica_groups=mesh['row'=32,'col'=8] {'col'}, dimensions={0}, use_global_device_ids=true | all-gather | bytes 46080 | tf_op jit(solution)/shard_map/all_gather | solution.py:19
  228.7 1.1 fusion.107
  233.3 1.1 slice_bitcast_fusion
  234.8 5.0 %slice.66 = f32[7,2,16,2,4,5,128]{6,2,5,4,3,1,0:T(8,128)} slice(f32[8,2,16,2,4,5,128]{6,2,5,4,3,1,0:T(8,128)} %all-gather.4.cloned.1.call-done), slice={[1:8], [0:2], [0:16], [0:2], [0:4], [0:5], [0:128]} | slice | bytes 9175040 | tf_op jit(solution)/shard_map/slice | solution.py:21
  239.8 16.7 %while.14 = (s32[]{:T(128)}, f32[2,16,2,4,5]{1,3,4,2,0:T(4,128)S(1)}, f32[2,16,2,4,5]{1,3,4,2,0:T(4,128)S(1)}, f32[2,16,2,4,5,128]{5,4,3,2,1,0:T(8,128)S(1)}, f3...) while((s32[]{:T(128)}, ...), condition=%wide.region_9.10_spmd, body=%wide.region_8.9_spmd.sunk | while | flops 499202 | bytes 3348581 | solution.py:22
  240.2 1.1 constant_dynamic-slice_fusion.3
  242.6 1.1 constant_dynamic-slice_fusion.3
  245.0 1.1 constant_dynamic-slice_fusion.3
  247.4 1.1 constant_dynamic-slice_fusion.3
  249.8 1.1 constant_dynamic-slice_fusion.3
  252.2 1.1 constant_dynamic-slice_fusion.3
  254.6 1.1 constant_dynamic-slice_fusion.3
  256.9 2.1 fusion.55
  (115 shorter events, 22.1 us)
Async XLA Ops:
  6.5 1.0 copy-start
  6.5 4.6 %copy-start.5 = (bf16[1,16,128,512]{3,2,1,0:T(8,128)(2,1)S(1)}, bf16[1,16,128,512]{3,2,1,0:T(8,128)(2,1)}, u32[]{:S(2)}) copy-start(bf16[1,16,128,512]{3,2,1,0:T(8,128)(2,1)} %param.15) | copy-start | bytes 6291460
  6.5 96.9 %reduce-scatter.2.cloned.1.call-start = ((), (), s32[]{:S(2)}) async-start(), calls=%async_computation.1 | async-start | bytes 4325376 | tf_op jit(solution)/shard_map/reduce_scatter | solution.py:73
  11.1 222.2 %all-gather.4.cloned.1.call-start = ((), (), s32[]{:S(2)}) async-start(), calls=%async_computation.2 | async-start | bytes 5898240 | tf_op jit(solution)/shard_map/all_gather | solution.py:19
  11.2 6.1 %copy-start.12 = (s32[2,64]{1,0:T(2,128)S(1)}, s32[2,64]{1,0:T(2,128)}, u32[]{:S(2)}) copy-start(s32[2,64]{1,0:T(2,128)} %param.13) | copy-start | bytes 1540
  11.2 6.3 %copy-start.11 = (s32[2]{0:T(128)S(1)}, s32[2]{0:T(128)}, u32[]{:S(2)}) copy-start(s32[2]{0:T(128)} %param.14) | copy-start | bytes 28
  11.2 6.4 %copy-start.10 = (s32[2,16]{1,0:T(2,128)S(1)}, s32[2,16]{1,0:T(2,128)}, u32[]{:S(2)}) copy-start(s32[2,16]{1,0:T(2,128)} %param.17) | copy-start | bytes 388
  18.0 116.2 %copy-start.8 = (f32[2,16,2,64]{3,1,2,0:T(8,128)}, f32[2,16,2,64]{3,1,2,0:T(8,128)S(1)}, u32[]{:S(2)}) copy-start(f32[2,16,2,64]{3,1,2,0:T(8,128)S(1)} %get-tuple-element.124) | copy-start | bytes 49156
  18.0 116.2 %copy-start.9 = (f32[2,16,2,64]{3,1,2,0:T(8,128)}, f32[2,16,2,64]{3,1,2,0:T(8,128)S(1)}, u32[]{:S(2)}) copy-start(f32[2,16,2,64]{3,1,2,0:T(8,128)S(1)} %get-tuple-element.125) | copy-start | bytes 49156
  132.1 0.8 copy-start.6
  133.9 0.8 copy-start.1
  133.9 1.0 copy-start.3
  162.2 39.3 %copy-start.2 = (bf16[2,16,2,20,64]{4,3,1,2,0:T(8,128)(2,1)S(1)}, bf16[2,16,2,20,64]{4,3,1,2,0:T(8,128)(2,1)}, u32[]{:S(2)}) copy-start(bf16[2,16,2,20,64]{4,3,1,2,0:T(8,128)(2,1)} %copy-done.1) | copy-start | bytes 491524
  162.2 39.3 %copy-start.4 = (bf16[2,16,2,20,64]{4,3,1,2,0:T(8,128)(2,1)S(1)}, bf16[2,16,2,20,64]{4,3,1,2,0:T(8,128)(2,1)}, u32[]{:S(2)}) copy-start(bf16[2,16,2,20,64]{4,3,1,2,0:T(8,128)(2,1)} %copy-done.3) | copy-start | bytes 491524
  228.7 3.6 %copy-start.7 = (f32[8,2,16,2,4,5]{2,4,5,3,1,0:T(4,128)}, f32[8,2,16,2,4,5]{2,4,5,3,1,0:T(4,128)S(1)}, u32[]{:S(2)}) copy-start(f32[8,2,16,2,4,5]{2,4,5,3,1,0:T(4,128)S(1)} %all_gather.13) | copy-start | bytes 122884
  234.7 5.0 %slice-start = ((f32[8,2,16,2,4,5]{2,4,5,3,1,0:T(4,128)}), f32[7,2,16,2,4,5]{2,4,5,3,1,0:T(4,128)S(1)}, s32[]{:S(2)}) async-start(f32[8,2,16,2,4,5]{2,4,5,3,1,0:T(4,128)} %copy-done.7), calls=%async_computation.3 | async-start | bytes 573440 | tf_op jit(solution)/shard_map/slice | solution.py:21
Sparse Core Ops, SparseCore 0:
  11.3 92.0 reduce-scatter.1
  155.6 68.7 all-gather.3
where the time goes:
time: 268 us; the launch traced here: 267 us
  waiting for transfers between devices  85.4 us (32%)
  blocking collectives  78.7 us (29%)
  local copies, waits for them, and re-layouts  45.2 us (17%)
  matrix products  27.5 us (10%)
  other arithmetic  15.7 us (6%)
  between operations  13.8 us (5%)
    reduce_scatter x1, waiting for transfers between devices, local(): lax.psum_scatter(project_rows(hidden, w_qkv), 'row', scatter_dimension=0,...  85.4 us
    all_gather x2, blocking collectives, merged(): pieces = jax.tree.map(lambda part: lax.all_gather(part, axis), value)  51.9 us
    all_gather x1, blocking collectives, local(): projected = lax.all_gather(column_sums, 'col', axis=1, tiled=True)  26.7 us
    dynamic_slice x7, local copies, waits for them, and re-layouts, merged(): lax.scan(lambda total, section: (join(total, section), None), head, tail)  7.99 us
    dot_general x1, matrix products, local(): jnp.einsum('sr,sqkgd->rqkgd', owner_float, slot_acc, precision=lax.Precis...  7.38 us
    reduce_sum x1, other arithmetic, local(): slot_sums = jnp.sum(page_weights, axis=-1)  5.86 us
    dot_general x1, matrix products, local(): jnp.einsum('sqkgd,spkd->sqkgp', slot_queries, pool_keys.reshape(pool_slot...  5.66 us
    add x7, other arithmetic, combine_states(): acc_early * scale_early[..., None] + acc_late * scale_late[..., None]  5.49 us
  transfers between devices with their start and end apart: 2, of which 1 were waited for; matrix products, arithmetic and copies ran while one was open for 12% of the time, Pallas kernels for 0%

commit v1 on v0

v1 whole, which is shorter than its diff:
```python
import functools
import math

import jax
import jax.numpy as jnp
import numpy as np
from jax import lax
from jax.experimental import pallas as pl
from jax.experimental.pallas import tpu as pltpu
from jax.sharding import PartitionSpec as P

HEADS = 20
KVH = 4
GROUP = HEADS // KVH
HD = 128
NX = 4
NY = 4
NZ = 8
COLS = 448
WA = 256
WB = COLS - WA
KDEV = 80
CHIPS = NX * NY
TOK = 64
SLOTS = 16
PAGE = 128
KEYS = SLOTS * PAGE
TAIL = 512
CHUNK = 512
NCHUNK = KEYS // CHUNK
SCALE = 1.0 / math.sqrt(HD)
ROPE_BASE = 500000.0
LOW = -1e30
MESH = pl.DeviceIdType.MESH
F32 = jnp.float32
BF16 = jnp.bfloat16

W_COPIES = 8 + 2 + 3 * 4 + 4 * 2
H_COPIES = CHIPS - 1
Z_COPIES = 14
M_COPIES = 2 * (NZ - 1)
N_REMOTE = W_COPIES + H_COPIES + 1 + Z_COPIES + M_COPIES


def nt(a, b):
    return lax.dot_general(a, b, (((1,), (1,)), ((), ())), preferred_element_type=F32)


def iota(shape, axis):
    return lax.broadcasted_iota(jnp.int32, shape, axis)


def kernel(
    lengths,
    tails,
    table,
    freq,
    hidden_t,
    weights,
    page_keys,
    page_values,
    tail_keys,
    tail_values,
    out,
    hbuf,
    wa,
    wb,
    xsend,
    xrecv,
    zall,
    kbuf,
    vbuf,
    tkbuf,
    tvbuf,
    cosb,
    sinb,
    bias,
    tbias,
    qrot,
    qown,
    kvown,
    sbuf,
    pack,
    mlpack,
    racc,
    rml,
    send,
    recv,
    local,
):
    row = lax.axis_index("row")
    z = lax.axis_index("col")
    core = lax.rem(row, 2)
    chip = row // 2
    x = lax.rem(chip, NX)
    y = chip // NX
    first = core == 0

    def plane(a, b):
        dx = jnp.where(first, a, b)
        dy = jnp.where(first, b, a)
        there = lax.rem(y + dy, NY) * NX + lax.rem(x + dx, NX)
        return (there * 2 + core, z)

    def along(d):
        return (row, lax.rem(z + d, NZ))

    sibling = (chip * 2 + 1 - core, z)

    locals_ = []

    def fetch(source, target):
        copy = pltpu.make_async_copy(source, target, local.at[len(locals_)])
        copy.start()
        locals_.append(copy)
        return copy

    own_h = fetch(
        hidden_t.at[:, pl.ds(pl.multiple_of(chip * 128, 128), 128)], hbuf.at[pl.ds(0, KDEV)]
    )
    own_wa = fetch(weights.at[:, pl.ds(0, WA)], wa.at[0])
    own_wb = fetch(weights.at[:, pl.ds(WA, WB)], wb.at[0])

    barrier = pltpu.get_barrier_semaphore()
    for a in range(4):
        for b in range(4):
            if (a, b) != (0, 0):
                pl.semaphore_signal(barrier, inc=1, device_id=plane(a, b), device_id_type=MESH)
    pl.semaphore_signal(barrier, inc=1, device_id=sibling, device_id_type=MESH)
    for d in range(1, NZ):
        pl.semaphore_signal(barrier, inc=1, device_id=along(d), device_id_type=MESH)

    page_copies = []
    for k in range(KVH):
        lanes = pl.ds(k * HD, HD)
        page_copies.append(fetch(page_keys.at[0, :, :, lanes], kbuf.at[k]))
        page_copies.append(fetch(page_values.at[0, :, :, lanes], vbuf.at[k]))
    tail_copies = []
    for k in range(KVH):
        lanes = pl.ds(k * HD, HD)
        tail_copies.append(fetch(tail_keys.at[:, :, :, lanes], tkbuf.at[k]))
        tail_copies.append(fetch(tail_values.at[:, :, :, lanes], tvbuf.at[k]))

    pl.semaphore_wait(barrier, CHIPS + NZ - 1)

    remotes = []

    def push(source, target, device):
        at = len(remotes)
        copy = pltpu.make_async_remote_copy(
            src_ref=source,
            dst_ref=target,
            send_sem=send.at[at],
            recv_sem=recv.at[at],
            device_id=device,
            device_id_type=MESH,
        )
        copy.start()
        remotes.append(copy)
        return copy

    def at(a, b):
        return (a % 4) * 4 + (b % 4)

    def w_push(a, b, half, axis, step):
        da, db = (step, 0) if axis == 0 else (0, step)
        buffer = wa if half == 0 else wb
        there = at(a - da, b - db)
        source = buffer.at[at(a, b)]
        if (a, b) == (0, 0):
            source = weights.at[:, pl.ds(0, WA)] if half == 0 else weights.at[:, pl.ds(WA, WB)]
        return push(source, buffer.at[there], plane(da % 4, db % 4))

    got = {}
    for axis in (0, 1):
        for step in (1, -1):
            for half in (0, 1):
                got["own", axis, step, half] = w_push(0, 0, half, axis, step)
    h_copies = []
    for a, b in sorted(
        [(a, b) for a in range(4) for b in range(4) if (a, b) != (0, 0)],
        key=lambda ab: -(min(ab[0], 4 - ab[0]) + min(ab[1], 4 - ab[1])),
    ):
        device = plane(a, b)
        there = device[0] // 2
        h_copies.append(
            push(
                hidden_t.at[:, pl.ds(pl.multiple_of(there * 128, 128), 128)],
                hbuf.at[pl.ds(at(-a, -b) * KDEV, KDEV)],
                device,
            )
        )

    lane = iota((TOK, HD), 1)
    token = iota((TOK, HD), 0)
    position = jnp.zeros((TOK, HD), jnp.int32)
    for c in range(NZ):
        for p in range(2):
            for s in range(2):
                number = c * 4 + p * 2 + s
                value = lengths[p] + tails[p, 2 * c + s]
                position = jnp.where(token // 2 == number, value, position)
    position = position + lax.rem(token, 2)
    angles = position.astype(F32) * freq[...]
    cosb[...] = jnp.cos(angles).reshape(NZ, 8, HD)
    sines = jnp.sin(angles)
    sinb[...] = jnp.where(lane < HD // 2, -sines, sines).reshape(NZ, 8, HD)

    sub = iota((8, PAGE), 0)
    wide = iota((8, PAGE), 1)
    slot_ids = z * SLOTS + iota((SLOTS, 64), 0)
    starts = iota((SLOTS, 64), 1) * PAGE
    seen = []
    for p in range(2):
        hit = table[p : p + 1, :] == slot_ids
        count = jnp.clip(lengths[p] - starts, 0, PAGE)
        seen.append(jnp.sum(jnp.where(hit, count, 0).astype(F32), axis=1, keepdims=True))
    for j in range(SLOTS):
        limit = jnp.where(sub < 4, seen[0][j : j + 1, :], seen[1][j : j + 1, :])
        bias[:, j * PAGE : (j + 1) * PAGE] = jnp.where(wide.astype(F32) < limit, 0.0, LOW)
    tsub = iota((8, TAIL), 0)
    twide = iota((8, TAIL), 1)
    for p in range(2):
        for s in range(2):
            number = p * 2 + s
            count = tails[p, 2 * z + s]
            shown = (tsub // 2 == number) & (twide < count)
            tbias[:, number * TAIL : (number + 1) * TAIL] = jnp.where(shown, 0.0, LOW)

    def arrived(copy):
        copy.wait_recv()

    for step in (1, -1):
        from_a = -step
        for half in (0, 1):
            arrived(got["own", 0, step, half])
        relay_half = 0 if step == 1 else 1
        got["far", relay_half] = w_push(from_a, 0, relay_half, 0, step)
        for half in (0, 1):
            for up in (1, -1):
                got["col", from_a % 4, up, half] = w_push(from_a, 0, half, 1, up)
    for up in (1, -1):
        for half in (0, 1):
            arrived(got["own", 1, up, half])
        relay_half = 0 if up == 1 else 1
        got["relay", 0, relay_half] = w_push(0, -up, relay_half, 1, up)
    for half in (0, 1):
        arrived(got["far", half])
        for up in (1, -1):
            got["col", 2, up, half] = w_push(2, 0, half, 1, up)
    for a in (3, 1, 2):
        for up in (1, -1):
            for half in (0, 1):
                arrived(got["col", a, up, half])
            relay_half = 0 if up == 1 else 1
            got["relay", a, relay_half] = w_push(a, -up, relay_half, 1, up)
    for copy in h_copies:
        arrived(copy)
    own_h.wait()
    own_wa.wait()
    own_wb.wait()
    for a in (0, 3, 1, 2):
        for half in (0, 1):
            arrived(got["relay", a, half])

    new = iota((2 * TOK, 2 * TOK), 0)
    old = iota((2 * TOK, 2 * TOK), 1)
    wanted = (
        (new // 64) * 64
        + lax.rem(new // 4, 2) * 32
        + (lax.rem(new, 64) // 8) * 4
        + lax.rem(new, 4)
    )
    order = jnp.where(wanted == old, 1.0, 0.0).astype(BF16)
    rows = nt(order, hbuf[...]).astype(BF16)
    for half, buffer, width in ((0, wa, WA), (1, wb, WB)):
        part = jnp.dot(
            rows, buffer[...].reshape(CHIPS * KDEV, width), preferred_element_type=F32
        )
        xsend[:, :, half * WA : half * WA + width] = part.reshape(2, TOK, width)
    swap = push(xsend.at[1 - core], xrecv, sibling)
    arrived(swap)
    projected = (xsend[core] + xrecv[...]).astype(BF16)
    zall[z] = projected.reshape(2, TOK // 2, COLS)

    ring = {}

    def z_push(distance, up, part):
        block = lax.rem(z + NZ - up * distance, NZ)
        ring[distance + 1, up, part] = push(
            zall.at[block, part], zall.at[block, part], along(up % NZ)
        )

    for part in (0, 1):
        for up in (1, -1):
            z_push(0, up, part if up == 1 else 1 - part)
    for distance in (1, 2, 3):
        for part in (0, 1):
            for up in (1, -1):
                piece = part if up == 1 else 1 - part
                arrived(ring[distance, up, piece])
                if distance < 3 or part == 0:
                    z_push(distance, up, piece)
    arrived(ring[4, 1, 0])
    arrived(ring[4, -1, 1])

    def head_columns(h):
        begin = h * HD
        block, offset = begin // COLS, begin % COLS
        if offset + HD <= COLS:
            return zall[block, :, :, offset : offset + HD].reshape(TOK, HD)
        cut = COLS - offset
        return jnp.concatenate(
            [
                zall[block, :, :, offset:COLS].reshape(TOK, cut),
                zall[block + 1, :, :, 0 : HD - cut].reshape(TOK, HD - cut),
            ],
            axis=1,
        )

    cosine = cosb[...].reshape(TOK, HD)
    signed = sinb[...].reshape(TOK, HD)

    def turn(values, cosine, signed):
        return values * cosine + pltpu.roll(values, HD // 2, 1) * signed

    for h in range(HEADS):
        k, g = h // GROUP, h % GROUP
        turned = turn(head_columns(h).astype(F32), cosine, signed).astype(BF16)
        qrot[k, g * TOK : (g + 1) * TOK, :] = turned
        qown[h] = turned.astype(F32).reshape(NZ, 8, HD)
    for i in range(2 * KVH):
        kvown[i] = head_columns(HEADS + i).astype(F32).reshape(NZ, 8, HD)

    for copy in page_copies:
        copy.wait()

    lanes = iota((TOK, HD), 1)
    tops = jnp.full((TOK, HD), LOW, F32)
    sums = jnp.zeros((TOK, HD), F32)
    for k in range(KVH):
        query = qrot[k]
        best = jnp.full((GROUP * TOK, PAGE), LOW, F32)
        for i in range(NCHUNK):
            keys = kbuf[k, i * 4 : (i + 1) * 4].reshape(CHUNK, HD)
            scores = nt(query, keys) * SCALE
            scores = (
                scores.reshape(GROUP * NZ, 8, CHUNK)
                + bias[:, i * CHUNK : (i + 1) * CHUNK][None]
            ).reshape(GROUP * TOK, CHUNK)
            sbuf[i] = scores
            for n in range(CHUNK // PAGE):
                best = jnp.maximum(best, scores[:, n * PAGE : (n + 1) * PAGE])
        top = jnp.max(best, axis=1, keepdims=True)
        total = jnp.zeros((GROUP * TOK, PAGE), F32)
        acc = jnp.zeros((GROUP * TOK, HD), F32)
        for i in range(NCHUNK):
            e = jnp.exp(sbuf[i] - top)
            for n in range(CHUNK // PAGE):
                total = total + e[:, n * PAGE : (n + 1) * PAGE]
            acc = acc + jnp.dot(
                e.astype(BF16),
                vbuf[k, i * 4 : (i + 1) * 4].reshape(CHUNK, HD),
                preferred_element_type=F32,
            )
        total = jnp.sum(total, axis=1, keepdims=True)
        for g in range(GROUP):
            h = k * GROUP + g
            part = slice(g * TOK, (g + 1) * TOK)
            pack[:, :, h * HD : (h + 1) * HD] = acc[part].reshape(NZ, 8, HD).astype(BF16)
            tops = jnp.where(lanes == h, top[part], tops)
            sums = jnp.where(lanes == h, total[part], sums)
    mlpack[:, 0] = tops.reshape(NZ, 8, HD)
    mlpack[:, 1] = sums.reshape(NZ, 8, HD)

    states = []
    for d in (4, 3, 5, 2, 6, 1, 7):
        there = lax.rem(z + d, NZ)
        device = along(d)
        states.append(push(pack.at[there], racc.at[NZ - d], device))
        states.append(push(mlpack.at[there], rml.at[NZ - d], device))

    for copy in tail_copies:
        copy.wait()
    fresh_row = iota((8, 16), 0)
    fresh_col = iota((8, 16), 1)
    fresh_shown = (
        (fresh_col < 8)
        & (fresh_row // 2 == fresh_col // 2)
        & (lax.rem(fresh_col, 2) <= lax.rem(fresh_row, 2))
    )
    fresh_bias = jnp.where(fresh_shown, 0.0, LOW)
    nothing = jnp.zeros((8, HD), F32)
    my_cos = cosb[z]
    my_sin = sinb[z]
    small = iota((8, HD), 1)
    own_tops = jnp.full((8, HD), LOW, F32)
    own_sums = jnp.zeros((8, HD), F32)
    own_acc = []
    for k in range(KVH):
        query = jnp.concatenate([qown[k * GROUP + g, z] for g in range(GROUP)], axis=0)
        query = query.astype(BF16)
        new_key = turn(kvown[k, z], my_cos, my_sin)
        new_key = jnp.concatenate([new_key, nothing], axis=0).astype(BF16)
        new_value = jnp.concatenate([kvown[KVH + k, z], nothing], axis=0).astype(BF16)
        scores = nt(query, tkbuf[k].reshape(KEYS, HD)) * SCALE
        scores = scores.reshape(GROUP, 8, KEYS) + tbias[...][None]
        scores = scores.reshape(GROUP * 8, KEYS)
        fresh = nt(query, new_key) * SCALE
        fresh = (fresh.reshape(GROUP, 8, 16) + fresh_bias[None]).reshape(GROUP * 8, 16)
        top = jnp.maximum(
            jnp.max(scores, axis=1, keepdims=True), jnp.max(fresh, axis=1, keepdims=True)
        )
        e = jnp.exp(scores - top)
        f = jnp.exp(fresh - top)
        total = jnp.sum(e, axis=1, keepdims=True) + jnp.sum(f, axis=1, keepdims=True)
        acc = jnp.dot(
            e.astype(BF16), tvbuf[k].reshape(KEYS, HD), preferred_element_type=F32
        ) + jnp.dot(f.astype(BF16), new_value, preferred_element_type=F32)
        for g in range(GROUP):
            h = k * GROUP + g
            part = slice(g * 8, (g + 1) * 8)
            own_acc.append(acc[part])
            own_tops = jnp.where(small == h, top[part], own_tops)
            own_sums = jnp.where(small == h, total[part], own_sums)

    for copy in states:
        arrived(copy)
    racc[0] = pack[z]
    rml[0] = mlpack[z]
    best = own_tops
    for i in range(NZ):
        best = jnp.maximum(best, rml[i, 0])
    factors = [jnp.exp(own_tops - best)]
    total = factors[0] * own_sums
    for i in range(NZ):
        factor = jnp.exp(rml[i, 0] - best)
        factors.append(factor)
        total = total + factor * rml[i, 1]
    for h in range(HEADS):
        column = slice(h * HD, (h + 1) * HD)
        acc = factors[0][:, h : h + 1] * own_acc[h]
        for i in range(NZ):
            acc = acc + factors[i + 1][:, h : h + 1] * racc[i, :, column].astype(F32)
        out[:, column] = (acc / total[:, h : h + 1]).astype(BF16)

    for copy in remotes:
        copy.wait_send()


def local_step(
    hidden,
    w_qkv,
    page_table,
    prompt_lengths,
    page_keys,
    page_values,
    tail_lengths,
    tail_keys,
    tail_values,
):
    half = np.arange(HD // 2, dtype=np.float64)
    one = np.exp(half * (-2.0 * math.log(ROPE_BASE) / HD)).astype(np.float32)
    freq = jnp.asarray(np.concatenate([one, one])[None])
    smem = pl.BlockSpec(memory_space=pltpu.SMEM)
    vmem = pl.BlockSpec(memory_space=pltpu.VMEM)
    hbm = pl.BlockSpec(memory_space=pl.ANY)
    attended = pl.pallas_call(
        kernel,
        out_shape=jax.ShapeDtypeStruct((8, HEADS * HD), BF16),
        in_specs=[smem, smem, vmem, vmem] + [hbm] * 6,
        out_specs=vmem,
        scratch_shapes=[
            pltpu.VMEM((CHIPS * KDEV, 2 * TOK), BF16),
            pltpu.VMEM((CHIPS, KDEV, WA), BF16),
            pltpu.VMEM((CHIPS, KDEV, WB), BF16),
            pltpu.VMEM((2, TOK, COLS), F32),
            pltpu.VMEM((TOK, COLS), F32),
            pltpu.VMEM((NZ, 2, TOK // 2, COLS), BF16),
            pltpu.VMEM((KVH, SLOTS, PAGE, HD), BF16),
            pltpu.VMEM((KVH, SLOTS, PAGE, HD), BF16),
            pltpu.VMEM((KVH, 2, 2, TAIL, HD), BF16),
            pltpu.VMEM((KVH, 2, 2, TAIL, HD), BF16),
            pltpu.VMEM((NZ, 8, HD), F32),
            pltpu.VMEM((NZ, 8, HD), F32),
            pltpu.VMEM((8, KEYS), F32),
            pltpu.VMEM((8, KEYS), F32),
            pltpu.VMEM((KVH, GROUP * TOK, HD), BF16),
            pltpu.VMEM((HEADS, NZ, 8, HD), F32),
            pltpu.VMEM((2 * KVH, NZ, 8, HD), F32),
            pltpu.VMEM((NCHUNK, GROUP * TOK, CHUNK), F32),
            pltpu.VMEM((NZ, 8, HEADS * HD), BF16),
            pltpu.VMEM((NZ, 2, 8, HD), F32),
            pltpu.VMEM((NZ, 8, HEADS * HD), BF16),
            pltpu.VMEM((NZ, 2, 8, HD), F32),
            pltpu.SemaphoreType.DMA((N_REMOTE,)),
            pltpu.SemaphoreType.DMA((N_REMOTE,)),
            pltpu.SemaphoreType.DMA((3 + 4 * KVH,)),
        ],
        compiler_params=pltpu.CompilerParams(
            collective_id=0, has_side_effects=True, vmem_limit_bytes=56 << 20
        ),
        name="decode",
    )(
        prompt_lengths,
        tail_lengths,
        page_table,
        freq,
        hidden.T,
        w_qkv,
        page_keys,
        page_values,
        tail_keys,
        tail_values,
    )
    return attended.reshape(2, 2, 2, HEADS * HD)


def solution(mesh):
    in_specs = (
        P(None, "row"),
        P("row", "col"),
        P("row", None),
        P("row"),
        P("row", "col", None, None),
        P("row", "col", None, None),
        P("row", None),
        P("row", "col", None, None),
        P("row", "col", None, None),
    )
    out_specs = P("row", "col", None, None)
    return jax.shard_map(
        local_step, mesh=mesh, in_specs=in_specs, out_specs=out_specs, check_vma=False
    )
```

time: 268 us -> 59.3 us (0.22)
  the two profiles are of different devices: /device:TPU:6 before, /device:TPU:1 now
where the time goes in v1:
time: 59.3 us; the launch traced here: 59.2 us
  Pallas kernels  57.7 us (97%)
  local copies, waits for them, and re-layouts  1.42 us (2%)
    pallas_call x1, Pallas kernels, local_step(): pl.pallas_call(kernel, out_shape=jax.ShapeDtypeStruct((8, HEADS * HD), BF...  57.7 us
    reshape x1, local copies, waits for them, and re-layouts, local_step(): return attended.reshape(2, 2, 2, HEADS * HD)  1.42 us

profile of v1, /device:TPU:1, one launch (start us, length us, event | category | flops | bytes accessed | tf_op | source)
XLA Modules:
  0.0 59.2 jit_solution(16186859323938272613)
XLA Ops:
  0.0 57.7 %decode.1 = bf16[8,2560]{1,0:T(8,128)(2,1)} custom-call(s32[2]{0:T(128)} %lengths.1, s32[2,16]{1,0:T(2,128)} %tails.1, s32[2,64]{1,0:T(2,128)} %table.1, f32[1,128]{1,0:T(1,128)} %constant.2.clone.freq, bf16[80,2048]{1,0:T(8,128)(2,1)} %bitcast.1, bf16[80,448]{1,0:T(8,128)(2,1)} %weights.1, bf16[1,16,128,512]{3,2,1,0:T(8,128)(2,1)} %page_keys.1, ...), custom_call_target="tpu_custom_call" | custom-call | tf_op jit(solution)/shard_map/decode/pallas_call | solution.py:468
  57.7 1.4 %reshape.3 = bf16[2,2,2,2560]{3,2,1,0:T(2,128)(2,1)} reshape(bf16[8,2560]{1,0:T(8,128)(2,1)} %decode.1) | data formatting | bytes 81920 | tf_op jit(solution)/shard_map/reshape | solution.py:516

commit v2 on v1

--- a/solution.py
+++ b/solution.py
@@ -37,8 +37,11 @@
 
 W_COPIES = 8 + 2 + 3 * 4 + 4 * 2
 H_COPIES = CHIPS - 1
-Z_COPIES = 14
-M_COPIES = 2 * (NZ - 1)
+PARTS = 2
+ROWS = TOK // PARTS
+Z_COPIES = 7 * PARTS
+KCOLS = GROUP * HD
+M_COPIES = (KVH // 2 + 1) * (NZ - 1)
 N_REMOTE = W_COPIES + H_COPIES + 1 + Z_COPIES + M_COPIES
 
 
@@ -281,7 +284,7 @@
     swap = push(xsend.at[1 - core], xrecv, sibling)
     arrived(swap)
     projected = (xsend[core] + xrecv[...]).astype(BF16)
-    zall[z] = projected.reshape(2, TOK // 2, COLS)
+    zall[z] = projected.reshape(PARTS, ROWS, COLS)
 
     ring = {}
 
@@ -291,18 +294,22 @@
             zall.at[block, part], zall.at[block, part], along(up % NZ)
         )
 
-    for part in (0, 1):
+    def piece_of(part, up):
+        return part if up == 1 else (part + PARTS // 2) % PARTS
+
+    for part in range(PARTS):
         for up in (1, -1):
-            z_push(0, up, part if up == 1 else 1 - part)
+            z_push(0, up, piece_of(part, up))
     for distance in (1, 2, 3):
-        for part in (0, 1):
+        for part in range(PARTS):
             for up in (1, -1):
-                piece = part if up == 1 else 1 - part
+                piece = piece_of(part, up)
                 arrived(ring[distance, up, piece])
-                if distance < 3 or part == 0:
+                if distance < 3 or part < PARTS // 2:
                     z_push(distance, up, piece)
-    arrived(ring[4, 1, 0])
-    arrived(ring[4, -1, 1])
+    for part in range(PARTS // 2):
+        for up in (1, -1):
+            arrived(ring[4, up, piece_of(part, up)])
 
     def head_columns(h):
         begin = h * HD
@@ -335,10 +342,12 @@
     for copy in page_copies:
         copy.wait()
 
+    states = []
     lanes = iota((TOK, HD), 1)
-    tops = jnp.full((TOK, HD), LOW, F32)
-    sums = jnp.zeros((TOK, HD), F32)
-    for k in range(KVH):
+    mlpack[...] = jnp.full((NZ, 8, HD), LOW, F32)
+
+    def attend(k):
+        both = mlpack[...].reshape(TOK, HD)
         query = qrot[k]
         best = jnp.full((GROUP * TOK, PAGE), LOW, F32)
         for i in range(NCHUNK):
@@ -368,18 +377,22 @@
             h = k * GROUP + g
             part = slice(g * TOK, (g + 1) * TOK)
             pack[:, :, h * HD : (h + 1) * HD] = acc[part].reshape(NZ, 8, HD).astype(BF16)
-            tops = jnp.where(lanes == h, top[part], tops)
-            sums = jnp.where(lanes == h, total[part], sums)
-    mlpack[:, 0] = tops.reshape(NZ, 8, HD)
-    mlpack[:, 1] = sums.reshape(NZ, 8, HD)
-
-    states = []
+            both = jnp.where(lanes == h, top[part], both)
+            both = jnp.where(lanes == h + HD // 2, total[part], both)
+        mlpack[...] = both.reshape(NZ, 8, HD)
+
+    for k in range(KVH):
+        pl.when(z >= 0)(functools.partial(attend, k))
+        if k % 2 == 0:
+            continue
+        columns = pl.ds((k - 1) * KCOLS, 2 * KCOLS)
+        for d in (4, 3, 5, 2, 6, 1, 7):
+            there = lax.rem(z + d, NZ)
+            source = pack.at[there, :, columns]
+            states.append(push(source, racc.at[NZ - d, :, columns], along(d)))
     for d in (4, 3, 5, 2, 6, 1, 7):
         there = lax.rem(z + d, NZ)
-        device = along(d)
-        states.append(push(pack.at[there], racc.at[NZ - d], device))
-        states.append(push(mlpack.at[there], rml.at[NZ - d], device))
-
+        states.append(push(mlpack.at[there], rml.at[NZ - d], along(d)))
     for copy in tail_copies:
         copy.wait()
     fresh_row = iota((8, 16), 0)
@@ -430,13 +443,13 @@
     rml[0] = mlpack[z]
     best = own_tops
     for i in range(NZ):
-        best = jnp.maximum(best, rml[i, 0])
+        best = jnp.maximum(best, rml[i])
     factors = [jnp.exp(own_tops - best)]
     total = factors[0] * own_sums
     for i in range(NZ):
-        factor = jnp.exp(rml[i, 0] - best)
+        factor = jnp.exp(rml[i] - best)
         factors.append(factor)
-        total = total + factor * rml[i, 1]
+        total = total + factor * pltpu.roll(rml[i], HD // 2, 1)
     for h in range(HEADS):
         column = slice(h * HD, (h + 1) * HD)
         acc = factors[0][:, h : h + 1] * own_acc[h]
@@ -476,7 +489,7 @@
             pltpu.VMEM((CHIPS, KDEV, WB), BF16),
             pltpu.VMEM((2, TOK, COLS), F32),
             pltpu.VMEM((TOK, COLS), F32),
-            pltpu.VMEM((NZ, 2, TOK // 2, COLS), BF16),
+            pltpu.VMEM((NZ, PARTS, ROWS, COLS), BF16),
             pltpu.VMEM((KVH, SLOTS, PAGE, HD), BF16),
             pltpu.VMEM((KVH, SLOTS, PAGE, HD), BF16),
             pltpu.VMEM((KVH, 2, 2, TAIL, HD), BF16),
@@ -490,9 +503,9 @@
             pltpu.VMEM((2 * KVH, NZ, 8, HD), F32),
             pltpu.VMEM((NCHUNK, GROUP * TOK, CHUNK), F32),
             pltpu.VMEM((NZ, 8, HEADS * HD), BF16),
-            pltpu.VMEM((NZ, 2, 8, HD), F32),
+            pltpu.VMEM((NZ, 8, HD), F32),
             pltpu.VMEM((NZ, 8, HEADS * HD), BF16),
-            pltpu.VMEM((NZ, 2, 8, HD), F32),
+            pltpu.VMEM((NZ, 8, HD), F32),
             pltpu.SemaphoreType.DMA((N_REMOTE,)),
             pltpu.SemaphoreType.DMA((N_REMOTE,)),
             pltpu.SemaphoreType.DMA((3 + 4 * KVH,)),

time: 59.3 us -> 58.3 us (0.983)
  Pallas kernels: 57.7 us -> 56.7 us
    pallas_call x1, Pallas kernels: 57.7 us -> 56.7 us  [local_step(): pl.pallas_call(kernel, out_shape=jax.ShapeDtypeStruct((8, HEADS * HD), BF...]
where the time goes in v2:
time: 58.3 us; the launch traced here: 58.1 us
  Pallas kernels  56.7 us (97%)
  local copies, waits for them, and re-layouts  1.42 us (2%)
    pallas_call x1, Pallas kernels, local_step(): pl.pallas_call(kernel, out_shape=jax.ShapeDtypeStruct((8, HEADS * HD), BF...  56.7 us
    reshape x1, local copies, waits for them, and re-layouts, local_step(): return attended.reshape(2, 2, 2, HEADS * HD)  1.42 us

profile of v2, /device:TPU:1, one launch (start us, length us, event | category | flops | bytes accessed | tf_op | source)
XLA Modules:
  0.0 58.1 jit_solution(1054680186747886720)
XLA Ops:
  0.0 56.7 %decode.1 = bf16[8,2560]{1,0:T(8,128)(2,1)} custom-call(s32[2]{0:T(128)} %lengths.1, s32[2,16]{1,0:T(2,128)} %tails.1, s32[2,64]{1,0:T(2,128)} %table.1, f32[1,128]{1,0:T(1,128)} %constant.2.clone.freq, bf16[80,2048]{1,0:T(8,128)(2,1)} %bitcast.1, bf16[80,448]{1,0:T(8,128)(2,1)} %weights.1, bf16[1,16,128,512]{3,2,1,0:T(8,128)(2,1)} %page_keys.1, ...), custom_call_target="tpu_custom_call" | custom-call | tf_op jit(solution)/shard_map/decode/pallas_call | solution.py:481
  56.7 1.4 %reshape.3 = bf16[2,2,2,2560]{3,2,1,0:T(2,128)(2,1)} reshape(bf16[8,2560]{1,0:T(8,128)(2,1)} %decode.1) | data formatting | bytes 81920 | tf_op jit(solution)/shard_map/reshape | solution.py:529

commit v3 on v2

--- a/solution.py
+++ b/solution.py
@@ -42,7 +42,7 @@
 Z_COPIES = 7 * PARTS
 KCOLS = GROUP * HD
 M_COPIES = (KVH // 2 + 1) * (NZ - 1)
-N_REMOTE = W_COPIES + H_COPIES + 1 + Z_COPIES + M_COPIES
+N_REMOTE = W_COPIES + H_COPIES + 2 + Z_COPIES + M_COPIES
 
 
 def nt(a, b):
@@ -276,13 +276,16 @@
     )
     order = jnp.where(wanted == old, 1.0, 0.0).astype(BF16)
     rows = nt(order, hbuf[...]).astype(BF16)
+    swaps = []
     for half, buffer, width in ((0, wa, WA), (1, wb, WB)):
         part = jnp.dot(
             rows, buffer[...].reshape(CHIPS * KDEV, width), preferred_element_type=F32
         )
         xsend[:, :, half * WA : half * WA + width] = part.reshape(2, TOK, width)
-    swap = push(xsend.at[1 - core], xrecv, sibling)
-    arrived(swap)
+        columns = pl.ds(half * WA, width)
+        swaps.append(push(xsend.at[1 - core, :, columns], xrecv.at[:, columns], sibling))
+    for copy in swaps:
+        arrived(copy)
     projected = (xsend[core] + xrecv[...]).astype(BF16)
     zall[z] = projected.reshape(PARTS, ROWS, COLS)
 

time: 58.3 us -> 59 us (1.012)
  Pallas kernels: 56.7 us -> 57.5 us
    pallas_call x1, Pallas kernels: 56.7 us -> 57.5 us  [local_step(): pl.pallas_call(kernel, out_shape=jax.ShapeDtypeStruct((8, HEADS * HD), BF...]
where the time goes in v3:
time: 59 us; the launch traced here: 58.9 us
  Pallas kernels  57.5 us (97%)
  local copies, waits for them, and re-layouts  1.42 us (2%)
    pallas_call x1, Pallas kernels, local_step(): pl.pallas_call(kernel, out_shape=jax.ShapeDtypeStruct((8, HEADS * HD), BF...  57.5 us
    reshape x1, local copies, waits for them, and re-layouts, local_step(): return attended.reshape(2, 2, 2, HEADS * HD)  1.42 us

profile of v3, /device:TPU:1, one launch (start us, length us, event | category | flops | bytes accessed | tf_op | source)
XLA Modules:
  0.0 58.9 jit_solution(11126148478516123038)
XLA Ops:
  0.0 57.5 %decode.1 = bf16[8,2560]{1,0:T(8,128)(2,1)} custom-call(s32[2]{0:T(128)} %lengths.1, s32[2,16]{1,0:T(2,128)} %tails.1, s32[2,64]{1,0:T(2,128)} %table.1, f32[1,128]{1,0:T(1,128)} %constant.2.clone.freq, bf16[80,2048]{1,0:T(8,128)(2,1)} %bitcast.1, bf16[80,448]{1,0:T(8,128)(2,1)} %weights.1, bf16[1,16,128,512]{3,2,1,0:T(8,128)(2,1)} %page_keys.1, ...), custom_call_target="tpu_custom_call" | custom-call | tf_op jit(solution)/shard_map/decode/pallas_call | solution.py:484
  57.5 1.4 %reshape.3 = bf16[2,2,2,2560]{3,2,1,0:T(2,128)(2,1)} reshape(bf16[8,2560]{1,0:T(8,128)(2,1)} %decode.1) | data formatting | bytes 81920 | tf_op jit(solution)/shard_map/reshape | solution.py:532
